TPU v7x, 32 devices: a whole 2x2x4 slice. The times are simulated.
32 devices in a mesh: blk: 16 (over z, x, core), grp: 2 (over y).
Axes of the slice: x: 2, y: 2, z: 4, core: 2. Of those that a mesh axis runs over, the one named last changes fastest.
Arguments:
- amplitudes: bfloat16 [16, 2, 16, 3, 128, 128], P('blk', 'grp'), may hold values from -6 to 6
- integral_slabs: bfloat16 [2, 2048, 512], P('grp', 'blk'), may hold values from -0.125 to 0.125
- tile_tasks: int32 [16, 2, 16, 3], P('blk', 'grp'), may hold values from -1 to 47, as said below
- owner_map: int32 [48], replicated, may hold values from 0 to 47, as said below
Outputs:
- residual: float32 [6144, 512], P('blk', 'grp')
Inputs may be any that keep to these rules, and one draw needn't show every extreme that they name: For a live entry I = tile_tasks[b, g, s, m], owner_map[I] // 3 == b; the live entries of one [b, g, s] are distinct and occupy its first slots; every [b, g] has at least one slab whose 3 slots are all live. `owner_map`: A permutation of the ij tiles.
All inputs are finite; a program needn't handle non-finite values.
Results may differ from a plain program's by a relative error of at most 0.0003.
Values may be sent and summed in bfloat16 or wider, within the bound.
A program may use at most 128 MiB of HBM per device.

v0:
```python
import jax
import jax.numpy as jnp
from jax import lax
from jax.sharding import PartitionSpec as P

HOLD = 3


def per_device(amplitudes, integral_slabs, tile_tasks, owner_map):
    amp_tiles = amplitudes[0, 0]
    task_list = tile_tasks[0, 0]
    tile_rows = amp_tiles.shape[2]
    count_tiles = owner_map.shape[0]
    row_base = lax.axis_index("blk") * HOLD
    matches = task_list[:, :, None] == jnp.arange(count_tiles, dtype=jnp.int32)
    owners = jnp.sum(jnp.where(matches, owner_map, 0), axis=2)
    local_row = owners - row_base
    live_slot = task_list >= 0
    hold_iota = jnp.arange(HOLD, dtype=jnp.int32)
    select = (live_slot[:, :, None] & (local_row[:, :, None] == hold_iota)).astype(jnp.bfloat16)
    gathered = lax.all_gather(integral_slabs, "blk", axis=1, tiled=True)
    dense_tiles = jnp.einsum(
        "smh,smrc->hrsc", select, amp_tiles, preferred_element_type=jnp.float32
    )
    dense_tiles = dense_tiles.astype(jnp.bfloat16).reshape(HOLD * tile_rows, -1)
    partial_value = jnp.dot(dense_tiles, gathered[0], preferred_element_type=jnp.float32)
    return lax.psum_scatter(partial_value, "grp", scatter_dimension=1, tiled=True)


def solution(mesh):
    placed = (
        P("blk", "grp", None, None, None, None),
        P("grp", "blk", None),
        P("blk", "grp", None, None),
        P(),
    )
    return jax.shard_map(
        per_device, mesh=mesh, in_specs=placed, out_specs=P("blk", "grp"), check_vma=False
    )
```

profile of v0, /device:TPU:0, one launch (start us, length us, event | category | flops | bytes accessed | tf_op | source)
XLA Modules:
  0.0 80.4 jit_solution(5856583974311549185)
XLA Ops:
  6.5 0.0 copy-start
  6.5 0.0 all-gather.2.cloned.1.call-start
  6.5 0.7 all-gather.2.cloned.1.call-update
  7.3 0.0 reduce-scatter.2.cloned.1.call-start
  7.3 0.7 copy.30
  8.0 0.9 %select_reduce_fusion = s32[16,3]{0,1:T(4,128)S(1)} fusion(s32[48]{0:T(128)} %param.7, s32[16,3]{0,1:T(4,128)S(1)} %bitcast.23), kind=kLoop, calls=%fused_computation.10 | loop fusion | flops 6864 | bytes 576 | tf_op jit(solution)/shard_map/reduce_sum | solution.py:16
  8.9 0.1 copy.13
  9.0 0.7 broadcast_compare_fusion
  9.6 0.1 copy.12
  9.7 0.0 copy-done
  9.7 1.5 %convert_bitcast_fusion = bf16[3,128,16,128]{3,0,1,2:T(4,128)(2,1)S(1)} fusion(bf16[16,3,128,128]{3,2,1,0:T(8,128)(2,1)S(1)} %bitcast.21, s32[16,3]{1,0:T(8,128)S(1)} %copy.13, pred[16,3]{1,0:T(8,128)(4,1)S(1)} %copy.12), kind=kOutput, calls=%fused_computation.4 | convolution fusion | flops 5505312 | bytes 3145968 | tf_op jit(solution)/shard_map/smh,smrc->hrsc/dot_general | solution.py:22
  11.2 1.3 %copy.15 = bf16[3,128,16,128]{3,2,1,0:T(8,128)(2,1)S(1)} copy(bf16[3,128,16,128]{3,0,1,2:T(4,128)(2,1)S(1)} %convert_bitcast_fusion) | data formatting | bytes 3145728 | tf_op jit(solution)/shard_map/convert_element_type | solution.py:25
  12.5 41.2 %all-gather.2.cloned.1.call-done = bf16[1,2048,512]{2,1,0:T(8,128)(2,1)} async-done(((bf16[1,128,512]{2,1,0:T(8,128)(2,1)}), bf16[1,2048,512]{2,1,0:T(8,128)(2,1)}) %all-gather.2.cloned.1.call-update) | async-done | bytes 2097168 | tf_op jit(solution)/shard_map/all_gather | solution.py:21
  53.7 3.5 %fusion = f32[384,512]{1,0:T(8,128)} fusion(bf16[1,2048,512]{2,1,0:T(8,128)(2,1)} %all-gather.2.cloned.1.call-done, bf16[48,8,16,128]{3,2,1,0:T(8,128)(2,1)S(1)} %bitcast.22), kind=kOutput, calls=%fused_computation | convolution fusion | flops 805306368 | bytes 4456448 | tf_op jit(solution)/shard_map/dot_general | solution.py:26
  57.2 0.0 reduce-scatter.2.cloned.1.call-update
  57.2 16.4 %reduce-scatter.2.cloned.1.call-done = f32[384,256]{1,0:T(8,128)} async-done(((f32[384,512]{1,0:T(8,128)}), f32[384,256]{1,0:T(8,128)}) %reduce-scatter.2.cloned.1.call-update) | async-done | bytes 393232 | tf_op jit(solution)/shard_map/reduce_scatter | solution.py:27
  (1 shorter events, 0.0 us)
Async XLA Ops:
  6.5 3.2 %copy-start = (bf16[1,1,16,3,128,128]{5,4,3,2,1,0:T(8,128)(2,1)S(1)}, bf16[1,1,16,3,128,128]{5,4,3,2,1,0:T(8,128)(2,1)}, u32[]{:S(2)}) copy-start(bf16[1,1,16,3,128,128]{5,4,3,2,1,0:T(8,128)(2,1)} %param.4) | copy-start | bytes 4718596
  6.5 47.2 %all-gather.2.cloned.1.call-start = ((), (), s32[]{:S(2)}) async-start(), calls=%async_computation.1 | async-start | bytes 2228224 | tf_op jit(solution)/shard_map/all_gather | solution.py:21
  7.3 66.3 %reduce-scatter.2.cloned.1.call-start = ((), (), s32[]{:S(2)}) async-start(), calls=%async_computation.2 | async-start | bytes 1179648 | tf_op jit(solution)/shard_map/reduce_scatter | solution.py:27
Sparse Core Ops, SparseCore 0:
  9.5 44.1 all-gather.1
  57.3 16.2 reduce-scatter.1
where the time goes:
time: 80.6 us; the launch traced here: 80.4 us
  waiting for transfers between devices  58.3 us (72%)
  between operations  13.4 us (17%)
  matrix products  4.94 us (6%)
  local copies, waits for them, and re-layouts  2.16 us (3%)
  other arithmetic  1.56 us (2%)
    all_gather x1, waiting for transfers between devices, per_device(): gathered = lax.all_gather(integral_slabs, 'blk', axis=1, tiled=True)  41.2 us
    reduce_scatter x1, waiting for transfers between devices, per_device(): lax.psum_scatter(partial_value, 'grp', scatter_dimension=1, tiled=True)  16.4 us
    dot_general x1, matrix products, per_device(): jnp.dot(dense_tiles, gathered[0], preferred_element_type=jnp.float32)  3.48 us
  transfers between devices with their start and end apart: 2, of which 2 were waited for; matrix products, arithmetic and copies ran while one was open for 6% of the time, Pallas kernels for 0%

commit v1 on v0

v1 whole, which is shorter than its diff:
```python
import functools

import jax
import jax.numpy as jnp
from jax import lax
from jax.experimental import pallas as pl
from jax.experimental.pallas import tpu as pltpu
from jax.sharding import PartitionSpec as P

MESH = pl.DeviceIdType.MESH
LANES = 128
ROW = 2
CORES = 2


def for_range(low, high, body):
    if high - low <= 8:
        for i in range(low, high):
            body(i)
    else:
        pl.loop(low, high)(body)


def kernel(
    dims,
    tasks_ref,
    owner_ref,
    amp_hbm,
    slab_hbm,
    keep_ref,
    recv_ref,
    amp_ref,
    slabs,
    dense,
    outgoing,
    amp_sem,
    slab_sem,
    line_send,
    line_recv,
    row_send,
    row_recv,
    core_send,
    core_recv,
    sum_send,
    sum_recv,
):
    lines, hold, most, rows, depth, half = dims
    chunks = half // LANES
    steps = 2 * chunks
    me = lax.axis_index("blk")
    grp = lax.axis_index("grp")
    core = me % CORES
    row = (me // CORES) % ROW
    line = me // (CORES * ROW)

    def blk_of(z, x, c):
        return (z * ROW + x) * CORES + c

    def line_peer(i):
        return blk_of((line + i) % lines, row, core)

    row_peer = blk_of(line, 1 - row, core)
    core_peer = blk_of(line, row, 1 - core)

    def column(k):
        side = 1 - grp if k < chunks else grp
        return pl.multiple_of(side * half + (k % chunks) * LANES, LANES)

    loads = [
        pltpu.make_async_copy(
            slab_hbm.at[:, pl.ds(column(k), LANES)], slabs.at[k, 0, 0, 0], slab_sem.at[k]
        )
        for k in range(steps)
    ]
    for load in loads:
        load.start()
    amp_load = pltpu.make_async_copy(amp_hbm, amp_ref, amp_sem)
    amp_load.start()

    barrier = pltpu.get_barrier_semaphore()

    def greet(blk, g):
        pl.semaphore_signal(barrier, inc=1, device_id=(blk, g), device_id_type=MESH)

    for_range(1, lines, lambda i: greet(line_peer(i), grp))
    greet(row_peer, grp)
    greet(core_peer, grp)
    greet(me, 1 - grp)

    def line_copy(k, i):
        return pltpu.make_async_remote_copy(
            src_ref=slabs.at[k, 0, 0, 0],
            dst_ref=slabs.at[k, 0, i, 0],
            send_sem=line_send.at[k, i],
            recv_sem=line_recv.at[k, i],
            device_id=(line_peer(lines - i), grp),
            device_id_type=MESH,
        )

    def row_copy(k, i):
        return pltpu.make_async_remote_copy(
            src_ref=slabs.at[k, 0, i, 0],
            dst_ref=slabs.at[k, 1, i, 0],
            send_sem=row_send.at[k, i],
            recv_sem=row_recv.at[k, i],
            device_id=(row_peer, grp),
            device_id_type=MESH,
        )

    def core_copy(k, x, i):
        return pltpu.make_async_remote_copy(
            src_ref=slabs.at[k, x, i, 0],
            dst_ref=slabs.at[k, x, i, 1],
            send_sem=core_send.at[k, x, i],
            recv_sem=core_recv.at[k, x, i],
            device_id=(core_peer, grp),
            device_id_type=MESH,
        )

    def sum_copy(k, h):
        at = pl.ds(h * rows, rows)
        return pltpu.make_async_remote_copy(
            src_ref=outgoing.at[k, at],
            dst_ref=recv_ref.at[at, pl.ds(k * LANES, LANES)],
            send_sem=sum_send.at[k, h],
            recv_sem=sum_recv.at[k, h],
            device_id=(me, 1 - grp),
            device_id_type=MESH,
        )

    def line_sends(k):
        loads[k].wait()
        for_range(1, lines, lambda i: line_copy(k, i).start())

    def own_sends(k):
        row_copy(k, 0).start()
        core_copy(k, 0, 0).start()

    def line_arrivals(k):
        def arrive(i):
            line_copy(k, i).wait_recv()
            row_copy(k, i).start()
            core_copy(k, 0, i).start()

        for_range(1, lines, arrive)

    def row_arrivals(k):
        def arrive(i):
            row_copy(k, i).wait_recv()
            core_copy(k, 1, i).start()

        for_range(0, lines, arrive)

    def core_arrivals(k, x):
        for_range(0, lines, lambda i: core_copy(k, x, i).wait_recv())

    pl.semaphore_wait(barrier, lines + 2)
    for k in range(steps):
        line_sends(k)
        if k < 2:
            own_sends(k)

    amp_load.wait()
    for x in range(ROW):
        for c in range(CORES):

            def fill(i, x=x, c=c):
                source = blk_of(
                    (line + i) % lines,
                    (row + x) % ROW,
                    (core + c) % CORES,
                )
                tiles = []
                for m in range(most):
                    task = tasks_ref[m, 0, source]
                    local = owner_ref[jnp.maximum(task, 0)] - me * hold
                    tiles.append(jnp.where(task >= 0, local, -1))
                at = pl.multiple_of(((x * lines + i) * CORES + c) * depth, depth)
                for h in range(hold):
                    slot = jnp.int32(0)
                    live = jnp.int32(0)
                    for m in range(most):
                        hit = tiles[m] == h
                        slot = jnp.where(hit, m, slot)
                        live = jnp.where(hit, 1, live)
                    tile = amp_ref[source, slot]
                    dense[h * rows : (h + 1) * rows, pl.ds(at, depth)] = jnp.where(
                        live > 0, tile, jnp.zeros_like(tile)
                    )

            for_range(0, lines, fill)

    span = lines * CORES * depth

    def product(k, x):
        width = min(span, 2048)

        def term(j):
            first = pl.multiple_of(j * width, width)
            block = slabs[k, x, pl.ds(j * (width // (CORES * depth)), width // (CORES * depth))]
            return jnp.dot(
                dense[:, pl.ds(x * span + first, width)],
                block.reshape(width, LANES),
                preferred_element_type=jnp.float32,
            )

        if span == width:
            return term(0)
        zero = jnp.zeros((hold * rows, LANES), jnp.float32)
        return lax.fori_loop(0, span // width, lambda j, total: total + term(j), zero)

    def near(k):
        core_arrivals(k, 0)
        if k < chunks:
            outgoing[k] = product(k, 0)
        else:
            keep_ref[:, pl.ds((k - chunks) * LANES, LANES)] = product(k, 0)

    def far(k):
        core_arrivals(k, 1)
        if k < chunks:
            outgoing[k] += product(k, 1)
            for h in range(hold):
                sum_copy(k, h).start()
        else:
            keep_ref[:, pl.ds((k - chunks) * LANES, LANES)] += product(k, 1)

    line_arrivals(0)
    for k in range(steps):
        if k + 2 < steps:
            own_sends(k + 2)
        if k + 1 < steps:
            line_arrivals(k + 1)
        row_arrivals(k)
        near(k)
        far(k)

    for k in range(chunks):
        for h in range(hold):
            sum_copy(k, h).wait()
    for k in range(steps):
        for_range(1, lines, lambda i: line_copy(k, i).wait_send())

        def sent(i):
            row_copy(k, i).wait_send()
            for x in range(ROW):
                core_copy(k, x, i).wait_send()

        for_range(0, lines, sent)


def per_device(mesh, amplitudes, integral_slabs, tile_tasks, owner_map):
    amp = amplitudes[0, 0]
    slab = integral_slabs[0]
    count, most, rows, depth = amp.shape
    devices, groups = mesh.shape["blk"], mesh.shape["grp"]
    hold = owner_map.shape[0] // devices
    columns = slab.shape[1]
    half = columns // groups
    lines = devices // (ROW * CORES)
    chunks = half // LANES
    steps = groups * chunks
    dma = pltpu.SemaphoreType.DMA
    total = jax.ShapeDtypeStruct((hold * rows, half), jnp.float32)
    keep, recv = pl.pallas_call(
        functools.partial(kernel, (lines, hold, most, rows, depth, half)),
        out_shape=(total, total),
        in_specs=[
            pl.BlockSpec(memory_space=pltpu.SMEM),
            pl.BlockSpec(memory_space=pltpu.SMEM),
            pl.BlockSpec(memory_space=pl.ANY),
            pl.BlockSpec(memory_space=pl.ANY),
        ],
        out_specs=(
            pl.BlockSpec(memory_space=pltpu.VMEM),
            pl.BlockSpec(memory_space=pltpu.VMEM),
        ),
        scratch_shapes=[
            pltpu.VMEM(amp.shape, amp.dtype),
            pltpu.VMEM((steps, ROW, lines, CORES, depth, LANES), slab.dtype),
            pltpu.VMEM((hold * rows, count * depth), amp.dtype),
            pltpu.VMEM((chunks, hold * rows, LANES), jnp.float32),
            dma,
            dma((steps,)),
            dma((steps, lines)),
            dma((steps, lines)),
            dma((steps, lines)),
            dma((steps, lines)),
            dma((steps, ROW, lines)),
            dma((steps, ROW, lines)),
            dma((chunks, hold)),
            dma((chunks, hold)),
        ],
        compiler_params=pltpu.CompilerParams(
            collective_id=0, has_side_effects=True, vmem_limit_bytes=60 * 1024 * 1024
        ),
    )(tile_tasks[0].transpose(2, 0, 1), owner_map, amp, slab)
    return keep + recv


def solution(mesh):
    placed = (
        P("blk", "grp", None, None, None, None),
        P("grp", "blk", None),
        P("blk", "grp", None, None),
        P(),
    )
    return jax.shard_map(
        functools.partial(per_device, mesh),
        mesh=mesh,
        in_specs=placed,
        out_specs=P("blk", "grp"),
        check_vma=False,
    )
```

time: 80.6 us -> 32.9 us (0.41)
  waiting for transfers between devices: 58.3 us -> 0 us
  Pallas kernels: 0 us -> 30.8 us
  between operations: 13.4 us -> 0.01 us
  matrix products: 4.94 us -> 0 us
  local copies, waits for them, and re-layouts: 2.16 us -> 0 us
    all_gather x1 -> x0, waiting for transfers between devices: 41.2 us -> none  [per_device(): gathered = lax.all_gather(integral_slabs, 'blk', axis=1, tiled=True)]
    pallas_call x0 -> x1, Pallas kernels: none -> 30.8 us  [per_device(): pl.pallas_call(functools.partial(kernel, (lines, hold, most, rows, depth,...]
    reduce_scatter x1 -> x0, waiting for transfers between devices: 16.4 us -> none  [per_device(): lax.psum_scatter(partial_value, 'grp', scatter_dimension=1, tiled=True)]
    dot_general x2 -> x0, matrix products: 4.94 us -> none  [the longest x1 3.48 us: per_device(): jnp.dot(dense_tiles, gathered[0], preferred_element_type=jnp.float32)]
    add x0 -> x1, other arithmetic: none -> 1.91 us  [per_device(): return keep + recv]
    convert_element_type x1 -> x0, local copies, waits for them, and re-layouts: 1.29 us -> none  [per_device(): dense_tiles = dense_tiles.astype(jnp.bfloat16).reshape(HOLD * tile_rows, -1)]
    reduce_sum x1 -> x0, other arithmetic: 0.86 us -> none  [per_device(): owners = jnp.sum(jnp.where(matches, owner_map, 0), axis=2)]
  transfers between devices with their start and end apart: 2 -> 0, of which waited for: 2 -> 0; matrix products, arithmetic and copies ran while one was open for 6% -> 0% of each run, Pallas kernels for 0% -> 0%
where the time goes in v1:
time: 32.9 us; the launch traced here: 32.8 us
  Pallas kernels  30.8 us (94%)
  other arithmetic  1.91 us (6%)
    pallas_call x1, Pallas kernels, per_device(): pl.pallas_call(functools.partial(kernel, (lines, hold, most, rows, depth,...  30.8 us
    add x1, other arithmetic, per_device(): return keep + recv  1.91 us

profile of v1, /device:TPU:0, one launch (start us, length us, event | category | flops | bytes accessed | tf_op | source)
XLA Modules:
  0.0 32.8 jit_solution(16208559403605026924)
XLA Ops:
  0.0 30.8 %shard_map.46 = (f32[384,256]{1,0:T(8,128)}, f32[384,256]{1,0:T(8,128)}) custom-call(s32[3,1,16]{2,1,0:T(1,128)} %bitcast.7, s32[48]{0:T(128)} %owner_ref.1, bf16[16,3,128,128]{3,2,1,0:T(8,128)(2,1)} %bitcast.5, bf16[128,512]{1,0:T(8,128)(2,1)} %bitcast.6), custom_call_target="tpu_custom_call" | custom-call | tf_op jit(solution)/shard_map/pallas_call | solution.py:265
  30.8 1.9 %add.3 = f32[384,256]{1,0:T(8,128)} add(f32[384,256]{1,0:T(8,128)} %get-tuple-element.7, f32[384,256]{1,0:T(8,128)} %get-tuple-element.8) | non-fusion elementwise | flops 98304 | bytes 1179648 | tf_op jit(solution)/shard_map/add | solution.py:298

commit v2 on v1

--- a/solution.py
+++ b/solution.py
@@ -130,35 +130,42 @@
 
     def line_sends(k):
         loads[k].wait()
-        for_range(1, lines, lambda i: line_copy(k, i).start())
+        for_range(1, lines, lambda i: line_copy(k, lines - i).start())
 
     def own_sends(k):
         row_copy(k, 0).start()
         core_copy(k, 0, 0).start()
 
+    def line_arrive(k, i):
+        line_copy(k, i).wait_recv()
+        row_copy(k, i).start()
+        core_copy(k, 0, i).start()
+
+    def row_arrive(k, i):
+        row_copy(k, i).wait_recv()
+        core_copy(k, 1, i).start()
+
     def line_arrivals(k):
+        for_range(1, lines, lambda i: line_arrive(k, i))
+
+    def row_arrivals(k):
+        for_range(0, lines, lambda i: row_arrive(k, i))
+
+    def both_arrivals(k):
         def arrive(i):
-            line_copy(k, i).wait_recv()
-            row_copy(k, i).start()
-            core_copy(k, 0, i).start()
+            line_arrive(k, i)
+            row_arrive(k - 1, i - 1)
 
         for_range(1, lines, arrive)
-
-    def row_arrivals(k):
-        def arrive(i):
-            row_copy(k, i).wait_recv()
-            core_copy(k, 1, i).start()
-
-        for_range(0, lines, arrive)
+        row_arrive(k - 1, lines - 1)
 
     def core_arrivals(k, x):
         for_range(0, lines, lambda i: core_copy(k, x, i).wait_recv())
 
     pl.semaphore_wait(barrier, lines + 2)
-    for k in range(steps):
+    for k in range(2):
         line_sends(k)
-        if k < 2:
-            own_sends(k)
+        own_sends(k)
 
     amp_load.wait()
     for x in range(ROW):
@@ -226,12 +233,16 @@
             keep_ref[:, pl.ds((k - chunks) * LANES, LANES)] += product(k, 1)
 
     line_arrivals(0)
-    for k in range(steps):
-        if k + 2 < steps:
-            own_sends(k + 2)
+    for k in range(1, steps):
         if k + 1 < steps:
-            line_arrivals(k + 1)
-        row_arrivals(k)
+            line_sends(k + 1)
+            own_sends(k + 1)
+        both_arrivals(k)
+        if k - 1 < chunks:
+            near(k - 1)
+            far(k - 1)
+    row_arrivals(steps - 1)
+    for k in range(chunks, steps):
         near(k)
         far(k)
 

time: 32.9 us -> 31.4 us (0.954)
  Pallas kernels: 30.8 us -> 29.3 us
    pallas_call x1, Pallas kernels: 30.8 us -> 29.3 us  [per_device(): pl.pallas_call(functools.partial(kernel, (lines, hold, most, rows, depth,...]
where the time goes in v2:
time: 31.4 us; the launch traced here: 31.2 us
  Pallas kernels  29.3 us (93%)
  other arithmetic  1.91 us (6%)
    pallas_call x1, Pallas kernels, per_device(): pl.pallas_call(functools.partial(kernel, (lines, hold, most, rows, depth,...  29.3 us
    add x1, other arithmetic, per_device(): return keep + recv  1.91 us

profile of v2, /device:TPU:0, one launch (start us, length us, event | category | flops | bytes accessed | tf_op | source)
XLA Modules:
  0.0 31.2 jit_solution(3187428446328985185)
XLA Ops:
  0.0 29.3 %shard_map.46 = (f32[384,256]{1,0:T(8,128)}, f32[384,256]{1,0:T(8,128)}) custom-call(s32[3,1,16]{2,1,0:T(1,128)} %bitcast.7, s32[48]{0:T(128)} %owner_ref.1, bf16[16,3,128,128]{3,2,1,0:T(8,128)(2,1)} %bitcast.5, bf16[128,512]{1,0:T(8,128)(2,1)} %bitcast.6), custom_call_target="tpu_custom_call" | custom-call | tf_op jit(solution)/shard_map/pallas_call | solution.py:276
  29.3 1.9 %add.3 = f32[384,256]{1,0:T(8,128)} add(f32[384,256]{1,0:T(8,128)} %get-tuple-element.7, f32[384,256]{1,0:T(8,128)} %get-tuple-element.8) | non-fusion elementwise | flops 98304 | bytes 1179648 | tf_op jit(solution)/shard_map/add | solution.py:309

commit v3 on v2

--- a/solution.py
+++ b/solution.py
@@ -249,6 +249,9 @@
     for k in range(chunks):
         for h in range(hold):
             sum_copy(k, h).wait()
+            at = pl.ds(h * rows, rows)
+            lanes = pl.ds(k * LANES, LANES)
+            keep_ref[at, lanes] += recv_ref[at, lanes]
     for k in range(steps):
         for_range(1, lines, lambda i: line_copy(k, i).wait_send())
 
@@ -273,20 +276,18 @@
     steps = groups * chunks
     dma = pltpu.SemaphoreType.DMA
     total = jax.ShapeDtypeStruct((hold * rows, half), jnp.float32)
-    keep, recv = pl.pallas_call(
+    return pl.pallas_call(
         functools.partial(kernel, (lines, hold, most, rows, depth, half)),
-        out_shape=(total, total),
+        out_shape=total,
         in_specs=[
             pl.BlockSpec(memory_space=pltpu.SMEM),
             pl.BlockSpec(memory_space=pltpu.SMEM),
             pl.BlockSpec(memory_space=pl.ANY),
             pl.BlockSpec(memory_space=pl.ANY),
         ],
-        out_specs=(
-            pl.BlockSpec(memory_space=pltpu.VMEM),
-            pl.BlockSpec(memory_space=pltpu.VMEM),
-        ),
+        out_specs=pl.BlockSpec(memory_space=pltpu.VMEM),
         scratch_shapes=[
+            pltpu.VMEM((hold * rows, half), jnp.float32),
             pltpu.VMEM(amp.shape, amp.dtype),
             pltpu.VMEM((steps, ROW, lines, CORES, depth, LANES), slab.dtype),
             pltpu.VMEM((hold * rows, count * depth), amp.dtype),
@@ -306,7 +307,6 @@
             collective_id=0, has_side_effects=True, vmem_limit_bytes=60 * 1024 * 1024
         ),
     )(tile_tasks[0].transpose(2, 0, 1), owner_map, amp, slab)
-    return keep + recv
 
 
 def solution(mesh):

time: 31.4 us -> 30.9 us (0.984)
  other arithmetic: 1.91 us -> 0 us
  local copies, waits for them, and re-layouts: 0 us -> 1.77 us
  Pallas kernels: 29.3 us -> 28.9 us
    add x1 -> x0, other arithmetic: 1.91 us -> none  [per_device(): return keep + recv]
    unnamed x0 -> x1, local copies, waits for them, and re-layouts: none -> 1.77 us
    pallas_call x1, Pallas kernels: 29.3 us -> 28.9 us  [per_device(): pl.pallas_call(functools.partial(kernel, (lines, hold, most, rows, depth,...]
where the time goes in v3:
time: 30.9 us; the launch traced here: 30.7 us
  Pallas kernels  28.9 us (94%)
  local copies, waits for them, and re-layouts  1.77 us (6%)
    pallas_call x1, Pallas kernels, per_device(): pl.pallas_call(functools.partial(kernel, (lines, hold, most, rows, depth,...  28.9 us
    unnamed x1, local copies, waits for them, and re-layouts  1.77 us

profile of v3, /device:TPU:0, one launch (start us, length us, event | category | flops | bytes accessed | tf_op | source)
XLA Modules:
  0.0 30.7 jit_solution(16553242805050645294)
XLA Ops:
  0.0 28.9 %shard_map.46 = f32[384,256]{1,0:T(8,128)} custom-call(s32[3,1,16]{2,1,0:T(1,128)} %bitcast.7, s32[48]{0:T(128)} %owner_ref.1, bf16[16,3,128,128]{3,2,1,0:T(8,128)(2,1)} %bitcast.5, bf16[128,512]{1,0:T(8,128)(2,1)} %bitcast.6), custom_call_target="tpu_custom_call" | custom-call | tf_op jit(solution)/shard_map/pallas_call | solution.py:279
  28.9 1.8 %copy.6 = f32[384,256]{1,0:T(8,128)} copy(f32[384,256]{1,0:T(8,128)} %shard_map.46) | data formatting | bytes 786432
